TPU v7x, 32 devices: a whole 2x2x4 slice. The times are simulated.
32 devices in a mesh: req: 8 (over z, x), head: 4 (over y, core).
Axes of the slice: x: 2, y: 2, z: 4, core: 2. Of those that a mesh axis runs over, the one named last changes fastest.
Arguments:
- residual_in: bfloat16 [1024, 1536], P(('req', 'head')), may hold values from -3 to 3
- attn_gain: bfloat16 [1536], replicated, may hold values from 0.099609375 to 1.8984375
- w_qkv: bfloat16 [1536, 8, 320], P(None, 'head'), may hold values from -0.15625 to 0.15625
- w_out: bfloat16 [1536, 1536], P('head'), may hold values from -0.41992188 to 0.41992188
- kv_cache: bfloat16 [1024, 8, 192, 128], P('req', 'head'), as said below
- lengths: int32 [1024], P('req'), may hold values from 1 to 192, as said below
- moe_gain: bfloat16 [1536], replicated, may hold values from 0.099609375 to 1.8984375
- w_router: bfloat16 [1536, 24], replicated
- routes: int32 [1024, 8], P(('req', 'head')), may hold values from 0 to 23, all different within a row; in each aligned block of 32 rows (0 to 31, 32 to 63, ...) at most 12 rows name the same one
- w_in: bfloat16 [24, 1536, 1024], P('req'), may hold values from -0.15625 to 0.15625
- w_down: bfloat16 [24, 512, 1536], P('req'), may hold values from -0.5 to 0.5
Outputs:
- layer_out: bfloat16 [1024, 1536], P(('req', 'head'))
- new_kv: bfloat16 [1024, 8, 128], P('req', 'head')
Inputs may be any that keep to these rules, and one draw needn't show every extreme that they name: `kv_cache`: each position holds its key in the first 64 entries and its value in the last 64. `lengths`: some request has exactly 192 cached positions. `routes`: each row names 8 different experts. Among the 32 rows of one device no expert is named more than 12 times, a bound that some block reaches.
All inputs are finite; a program needn't handle non-finite values.
Results may differ from a plain program's by a relative error of at most 0.017.
Values may be sent and summed in bfloat16 or wider, within the bound.
A program may use at most 128 MiB of HBM per device.

v0:
```python
import jax
import jax.numpy as jnp
from jax import lax
from jax.sharding import PartitionSpec as P

D = 1536
HEADS = 24
KV = 8
HD = 64
F = 512


EPSILON = 1e-06
THETA = 10000.0


def rms_scale(values, gain):
    wide = values.astype(jnp.float32)
    mean_square = jnp.mean(wide * wide, axis=-1, keepdims=True)
    return (wide * lax.rsqrt(mean_square + EPSILON) * gain.astype(jnp.float32)).astype(jnp.bfloat16)


def rotate(vectors, lengths):
    half = vectors.shape[-1] // 2
    index = jnp.arange(half).astype(jnp.float32)
    frequency = jnp.power(THETA, -2.0 * index / vectors.shape[-1])
    angle = lengths.astype(jnp.float32)[:, None] * frequency[None, :]
    cosine = jnp.cos(angle)[:, None, None, :]
    sine = jnp.sin(angle)[:, None, None, :]
    first = vectors[..., :half]
    second = vectors[..., half:]
    return jnp.concatenate(
        [first * cosine - second * sine, second * cosine + first * sine], axis=-1
    )


def project_heads(projected, lengths, group, head_size):
    blocks = projected.reshape(projected.shape[0], -1, group + 2, head_size)
    queries = rotate(blocks[:, :, :group], lengths).astype(jnp.bfloat16)
    new_keys = rotate(blocks[:, :, group : group + 1], lengths).astype(jnp.bfloat16)[:, :, 0]
    new_values = blocks[:, :, group + 1].astype(jnp.bfloat16)
    return (queries, new_keys, new_values)


def own_scores(queries, new_keys):
    product = queries.astype(jnp.float32) * new_keys.astype(jnp.float32)[:, :, None, :]
    return jnp.sum(product, axis=-1) * HD ** (-0.5)


def own_term(own_weight, new_values):
    own_prob = own_weight.astype(jnp.bfloat16).astype(jnp.float32)
    return own_prob[..., None] * new_values.astype(jnp.float32)[:, :, None, :]


def attend_full(queries, new_keys, new_values, cache, lengths):
    scores = jnp.einsum(
        "rkgd,rkld->rkgl", queries, cache[..., :HD], preferred_element_type=jnp.float32
    ) * HD ** (-0.5)
    own = own_scores(queries, new_keys)
    positions = jnp.arange(cache.shape[2])
    live = (positions[None, :] < lengths[:, None])[:, None, None, :]
    masked = jnp.where(live, scores, -1e30)
    peak = jnp.maximum(jnp.max(masked, axis=-1), own)
    weights = jnp.where(live, jnp.exp(masked - peak[..., None]), 0.0)
    own_weight = jnp.exp(own - peak)
    total = jnp.sum(weights, axis=-1) + own_weight
    probabilities = weights.astype(jnp.bfloat16)
    weighted = jnp.einsum(
        "rkgl,rkld->rkgd", probabilities, cache[..., HD:], preferred_element_type=jnp.float32
    )
    weighted = weighted + own_term(own_weight, new_values)
    return (weighted / total[..., None]).astype(jnp.bfloat16)


def local(
    residual_in,
    attn_gain,
    w_qkv,
    w_out,
    kv_cache,
    lengths,
    moe_gain,
    w_router,
    routes,
    w_in,
    w_down,
):
    group = HEADS // KV
    tok_rows = residual_in.shape[0]
    req_rows = lengths.shape[0]
    kv_local = w_qkv.shape[1]
    normed = rms_scale(residual_in, attn_gain)
    flat_weight = w_qkv.reshape(D, kv_local * (group + 2) * HD)
    projected = jnp.dot(
        lax.all_gather(normed, "head", axis=0, tiled=True),
        flat_weight,
        preferred_element_type=jnp.float32,
    )
    queries, new_keys, new_values = project_heads(projected, lengths, group, HD)
    new_kv = jnp.concatenate([new_keys, new_values], axis=-1)
    heads_out = attend_full(queries, new_keys, new_values, kv_cache, lengths)
    local_width = kv_local * group * HD
    attn_heads = heads_out.reshape(req_rows, local_width)
    attention = lax.psum_scatter(
        jnp.dot(attn_heads, w_out, preferred_element_type=jnp.float32).astype(jnp.bfloat16),
        "head",
        scatter_dimension=0,
        tiled=True,
    ).astype(jnp.float32)
    attended = (residual_in.astype(jnp.float32) + attention).astype(jnp.bfloat16)
    normed_moe = rms_scale(attended, moe_gain)
    logits = jnp.dot(normed_moe, w_router, preferred_element_type=jnp.float32)
    gates = jax.nn.softmax(jnp.take_along_axis(logits, routes, axis=1), axis=-1)
    top = routes.shape[1]
    experts_all = w_router.shape[1]
    owners = lax.axis_size("req")
    local_experts = w_in.shape[0]
    capacity = (tok_rows * top + experts_all - 1) // experts_all + 1
    chosen = routes.reshape(tok_rows * top)
    onehot = (chosen[:, None] == jnp.arange(experts_all)[None, :]).astype(jnp.int32)
    earlier = jnp.cumsum(onehot, axis=0) - onehot
    within = jnp.sum(earlier * onehot, axis=1)
    slots = chosen * capacity + within
    placed = (slots[:, None] == jnp.arange(experts_all * capacity)[None, :]).astype(jnp.bfloat16)
    source = jnp.repeat(normed_moe, top, axis=0)
    outgoing = jnp.einsum("ps,pd->sd", placed, source, preferred_element_type=jnp.float32).astype(
        jnp.bfloat16
    )
    outgoing = outgoing.reshape(owners, local_experts, capacity, D)
    both = jnp.einsum(
        "sjcd,jdf->sjcf",
        lax.all_to_all(outgoing, "req", split_axis=0, concat_axis=0, tiled=True),
        w_in,
        preferred_element_type=jnp.float32,
    )
    hidden = (jax.nn.silu(both[..., :F]) * both[..., F:]).astype(jnp.bfloat16)
    result = jnp.einsum(
        "sjcf,jfd->sjcd", hidden, w_down, preferred_element_type=jnp.float32
    ).astype(jnp.bfloat16)
    returned = lax.all_to_all(result, "req", split_axis=0, concat_axis=0, tiled=True)
    picked = jnp.take(returned.reshape(experts_all * capacity, D), slots, axis=0).reshape(
        tok_rows, top, D
    )
    mixed = jnp.sum(gates[:, :, None] * picked.astype(jnp.float32), axis=1)
    layer_out = (attended.astype(jnp.float32) + mixed).astype(jnp.bfloat16)
    return (layer_out, new_kv)


def solution(mesh):
    return jax.shard_map(
        local,
        mesh=mesh,
        in_specs=(
            P(("req", "head"), None),
            P(),
            P(None, "head", None),
            P("head", None),
            P("req", "head", None, None),
            P("req"),
            P(),
            P(),
            P(("req", "head"), None),
            P("req", None, None),
            P("req", None, None),
        ),
        out_specs=(P(("req", "head"), None), P("req", "head", None)),
        check_vma=False,
    )
```

profile of v0, /device:TPU:0, one launch (start us, length us, event | category | flops | bytes accessed | tf_op | source)
XLA Modules:
  0.0 164.2 jit_solution(350964640558112470)
XLA Ops:
  7.2 0.8 convert_element_type.116
  8.0 0.7 iota_compare_fusion.2
  8.8 1.0 fusion.46
  9.8 0.7 convert_element_type.114
  10.5 1.0 fusion.48
  11.5 7.9 %all_gather.3 = bf16[128,1536]{1,0:T(8,128)(2,1)S(1)} all-gather(bf16[32,1536]{1,0:T(8,128)(2,1)S(1)} %fusion.48), channel_id=1, replica_groups=mesh['req'=8,'head'=4] {'head'}, dimensions={0}, use_global_device_ids=true | all-gather | bytes 491520 | tf_op jit(solution)/shard_map/all_gather | solution.py:95
  19.4 0.7 fusion.42
  20.1 0.1 multiply_cosine_fusion
  20.4 0.8 copy.89
  21.1 0.2 copy.81
  21.3 12.0 %fusion.69 = (f32[128,2,3]{2,1,0:T(2,128)}, f32[128,2,3,192]{3,2,1,0:T(4,128)S(1)}) fusion(bf16[128,2,3,64]{3,2,1,0:T(4,128)(2,1)S(1)} %copy.81, bf16[128,2,192,128]{3,2,1,0:T(8,128)(2,1)} %param.15, pred[128,192]{1,0:T(8,128)(4,1)S(1)} %iota_compare_fusion.2), kind=kOutput, calls=%fused_computation.101 | convolution fusion | flops 19315968 | bytes 13298688 | tf_op jit(solution)/shard_map/rkgd,rkld->rkgl/dot_general | solution.py:56
  33.3 1.1 copy.85
  34.4 0.2 copy.86
  34.6 0.8 fusion.35
  35.6 0.8 copy.88
  36.4 0.8 copy.91
  37.2 9.9 %fusion.30 = bf16[128,2,3,64]{3,2,1,0:T(4,128)(2,1)} fusion(bf16[128,2,192,128]{3,2,1,0:T(8,128)(2,1)} %param.15, f32[128,2,3,192]{3,2,1,0:T(4,128)} %copy-done.3, f32[128,2,3]{2,1,0:T(2,128)S(1)} %copy.86, pred[128,192]{1,0:T(8,128)(4,1)S(1)} %iota_compare_fusion.2, f32[128,2,3]{2,1,0:T(2,128)} %copy.91, f32[128,2,64]{2,1,0:T(2,128)} %copy.89, ...), kind=kOutput, calls=%fused_computation.22 | convolution fusion | flops 19513344 | bytes 13370368 | tf_op jit(solution)/shard_map/rkgl,rkld->rkgd/dot_general | solution.py:68
  47.1 1.1 copy.92
  48.2 1.1 convolution_convert_fusion.1
  49.5 0.1 reshape.238
  49.6 0.1 eq.39
  49.7 0.6 reduce-window.6
  50.3 0.2 slice_reduce_fusion
  50.5 0.1 fusion.58
  50.6 20.7 %reduce-scatter.2.cloned.1.call-done = bf16[32,1536]{1,0:T(8,128)(2,1)} async-done(((bf16[128,1536]{1,0:T(8,128)(2,1)}), bf16[32,1536]{1,0:T(8,128)(2,1)}) %reduce-scatter.2.cloned.1.call-update) | async-done | bytes 98320 | tf_op jit(solution)/shard_map/reduce_scatter | solution.py:104
  71.3 1.0 fusion.50
  72.3 1.0 fusion.52
  73.3 0.5 convolution_convert_fusion
  73.9 1.2 reshape.241
  75.1 5.5 %all-to-all-start = ((bf16[8,3,12,1536]{3,2,1,0:T(8,128)(2,1)}), bf16[8,3,12,1536]{3,2,1,0:T(8,128)(2,1)S(1)}, u32[]{:S(2)}, u32[]{:S(2)}) async-start(bf16[8,3,12,1536]{3,2,1,0:T(8,128)(2,1)} %reshape.241), calls=%async_computation.1 | async-start | bytes 2359296 | tf_op jit(solution)/shard_map/all_to_all | solution.py:132
  80.7 0.1 mul.257
  80.8 28.4 %all-to-all-done = bf16[8,3,12,1536]{3,2,1,0:T(8,128)(2,1)S(1)} async-done(((bf16[8,3,12,1536]{3,2,1,0:T(8,128)(2,1)}), bf16[8,3,12,1536]{3,2,1,0:T(8,128)(2,1)S(1)}, u32[]{:S(2)}, u32[]{:S(2)}) %all-to-all-start) | async-done | bytes 884768 | tf_op jit(solution)/shard_map/all_to_all | solution.py:132
  109.1 5.1 %fusion.14 = f32[8,3,12,1024]{3,2,0,1:T(8,128)S(1)} fusion(bf16[3,1536,1024]{2,1,0:T(8,128)(2,1)} %param.20, bf16[8,3,12,1536]{3,2,1,0:T(8,128)(2,1)S(1)} %all-to-all-done), kind=kOutput, calls=%fused_computation.15 | convolution fusion | flops 905969664 | bytes 11501568 | tf_op jit(solution)/shard_map/sjcd,jdf->sjcf/dot_general | solution.py:130
  114.2 3.2 %fusion.11 = bf16[8,3,12,1536]{3,2,0,1:T(8,128)(2,1)S(1)} fusion(bf16[3,512,1536]{2,1,0:T(8,128)(2,1)} %param.21, f32[8,3,12,1024]{3,2,0,1:T(8,128)S(1)} %fusion.14), kind=kOutput, calls=%fused_computation.12 | convolution fusion | flops 454311936 | bytes 6782976 | tf_op jit(solution)/shard_map/sjcf,jfd->sjcd/dot_general | solution.py:137
  117.5 1.1 copy.101
  118.6 4.2 %all-to-all-start.1 = ((bf16[8,3,12,1536]{3,2,1,0:T(8,128)(2,1)}), bf16[8,3,12,1536]{3,2,1,0:T(8,128)(2,1)}, u32[]{:S(2)}, u32[]{:S(2)}) async-start(bf16[8,3,12,1536]{3,2,1,0:T(8,128)(2,1)} %copy.101), calls=%async_computation.2 | async-start | bytes 2359296 | tf_op jit(solution)/shard_map/all_to_all | solution.py:140
  122.9 0.1 reshape.251
  123.0 0.8 copy.102
  123.8 0.1 fusion.70
  123.9 2.0 %gather_fusion.1 = f32[256]{0:T(256)S(1)} fusion(f32[32,24]{0,1:T(8,128)S(1)} %fusion.70, s32[256]{0:T(256)S(1)} %reshape.251), kind=kCustom, calls=%fused_computation.1 | custom fusion | bytes 4096 | tf_op jit(solution)/shard_map/jit(take_along_axis)/gather | solution.py:113
  126.0 0.1 fusion.68
  126.1 0.2 fusion.63
  126.3 0.1 fusion.62
  126.4 24.8 %all-to-all-done.1 = bf16[8,3,12,1536]{3,2,1,0:T(8,128)(2,1)} async-done(((bf16[8,3,12,1536]{3,2,1,0:T(8,128)(2,1)}), bf16[8,3,12,1536]{3,2,1,0:T(8,128)(2,1)}, u32[]{:S(2)}, u32[]{:S(2)}) %all-to-all-start.1) | async-done | bytes 884768 | tf_op jit(solution)/shard_map/all_to_all | solution.py:140
  151.2 1.3 reshape.242
  152.5 2.1 %gather_fusion = bf16[256,1536]{1,0:T(8,128)(2,1)} fusion(bf16[288,1536]{1,0:T(8,128)(2,1)S(1)} %reshape.242, s32[1024]{0:T(1024)S(1)} %pad_clamp_fusion), kind=kCustom, calls=%fused_computation | custom fusion | bytes 1573888 | tf_op jit(solution)/shard_map/jit(_take)/gather | solution.py:141
  154.7 2.0 %multiply_reduce_fusion = f32[32,1536]{1,0:T(8,128)S(1)} fusion(bf16[256,1536]{1,0:T(8,128)(2,1)} %gather_fusion, f32[32,8]{1,0:T(8,128)S(1)} %fusion.62, pred[32,8]{1,0:T(8,128)(4,1)S(1)} %compare_and_fusion), kind=kLoop, calls=%fused_computation.14 | loop fusion | flops 1523712 | bytes 984320 | tf_op jit(solution)/shard_map/reduce_sum | solution.py:144
  156.7 0.7 fusion.53
  (44 shorter events, 0.7 us)
Async XLA Ops:
  7.2 12.3 %copy-start = (bf16[1536,2,320]{0,2,1:T(8,128)(2,1)S(1)}, bf16[1536,2,320]{0,2,1:T(8,128)(2,1)}, u32[]{:S(2)}) copy-start(bf16[1536,2,320]{0,2,1:T(8,128)(2,1)} %param.13) | copy-start | bytes 5898244
  7.2 64.1 %reduce-scatter.2.cloned.1.call-start = ((), (), s32[]{:S(2)}) async-start(), calls=%async_computation.3 | async-start | bytes 491520 | tf_op jit(solution)/shard_map/reduce_scatter | solution.py:104
  33.3 3.0 %copy-start.3 = (f32[128,2,3,192]{3,2,1,0:T(4,128)}, f32[128,2,3,192]{3,2,1,0:T(4,128)S(1)}, u32[]{:S(2)}) copy-start(f32[128,2,3,192]{3,2,1,0:T(4,128)S(1)} %get-tuple-element.21) | copy-start | bytes 1769476
  37.2 11.1 %copy-start.2 = (bf16[384,1536]{1,0:T(8,128)(2,1)S(1)}, bf16[384,1536]{1,0:T(8,128)(2,1)}, u32[]{:S(2)}) copy-start(bf16[384,1536]{1,0:T(8,128)(2,1)} %param.14) | copy-start | bytes 3538948
  47.1 2.3 %copy-start.6 = (s32[32,8]{0,1:T(8,128)S(1)}, s32[32,8]{0,1:T(8,128)}, u32[]{:S(2)}) copy-start(s32[32,8]{0,1:T(8,128)} %param.19) | copy-start | bytes 3076
  47.1 2.6 %copy-start.7 = (bf16[1536]{0:T(1024)(128)(2,1)S(1)}, bf16[1536]{0:T(1024)(128)(2,1)}, u32[]{:S(2)}) copy-start(bf16[1536]{0:T(1024)(128)(2,1)} %param.17) | copy-start | bytes 9220
  47.1 24.2 %copy-start.1 = (bf16[32,1536]{1,0:T(8,128)(2,1)S(1)}, bf16[32,1536]{1,0:T(8,128)(2,1)}, u32[]{:S(2)}) copy-start(bf16[32,1536]{1,0:T(8,128)(2,1)} %param.11) | copy-start | bytes 294916
  75.1 34.1 %all-to-all-start = ((bf16[8,3,12,1536]{3,2,1,0:T(8,128)(2,1)}), bf16[8,3,12,1536]{3,2,1,0:T(8,128)(2,1)S(1)}, u32[]{:S(2)}, u32[]{:S(2)}) async-start(bf16[8,3,12,1536]{3,2,1,0:T(8,128)(2,1)} %reshape.241), calls=%async_computation.1 | async-start | bytes 2359296 | tf_op jit(solution)/shard_map/all_to_all | solution.py:132
  117.4 6.3 %copy-start.5 = (bf16[1536,24]{0,1:T(8,128)(2,1)S(1)}, bf16[1536,24]{0,1:T(8,128)(2,1)}, u32[]{:S(2)}) copy-start(bf16[1536,24]{0,1:T(8,128)(2,1)} %param.18) | copy-start | bytes 221188
  118.6 32.6 %all-to-all-start.1 = ((bf16[8,3,12,1536]{3,2,1,0:T(8,128)(2,1)}), bf16[8,3,12,1536]{3,2,1,0:T(8,128)(2,1)}, u32[]{:S(2)}, u32[]{:S(2)}) async-start(bf16[8,3,12,1536]{3,2,1,0:T(8,128)(2,1)} %copy.101), calls=%async_computation.2 | async-start | bytes 2359296 | tf_op jit(solution)/shard_map/all_to_all | solution.py:140
  152.5 4.1 %copy-start.4 = (bf16[32,1536]{1,0:T(8,128)(2,1)S(1)}, bf16[32,1536]{1,0:T(8,128)(2,1)}, u32[]{:S(2)}) copy-start(bf16[32,1536]{1,0:T(8,128)(2,1)} %reduce-scatter.2.cloned.1.call-done) | copy-start | bytes 294916
Sparse Core Ops, SparseCore 0:
  49.5 21.7 reduce-scatter.1
where the time goes:
time: 165 us; the launch traced here: 164 us
  waiting for transfers between devices  73.8 us (45%)
  matrix products  32.6 us (20%)
  local copies, waits for them, and re-layouts  14.4 us (9%)
  between operations  14.3 us (9%)
  other arithmetic  11.2 us (7%)
  starting transfers between devices  9.81 us (6%)
  blocking collectives  7.94 us (5%)
    all_to_all x1, waiting for transfers between devices, local(): lax.all_to_all(outgoing, 'req', split_axis=0, concat_axis=0, tiled=True)  28.4 us
    all_to_all x1, waiting for transfers between devices, local(): lax.all_to_all(result, 'req', split_axis=0, concat_axis=0, tiled=True)  24.8 us
    reduce_scatter x1, waiting for transfers between devices, local(): lax.psum_scatter(jnp.dot(attn_heads, w_out, preferred_element_type=jnp.fl...  20.7 us
    dot_general x1, matrix products, attend_full(): jnp.einsum('rkgd,rkld->rkgl', queries, cache[..., :HD], preferred_element...  12 us
    dot_general x1, matrix products, attend_full(): jnp.einsum('rkgl,rkld->rkgd', probabilities, cache[..., HD:], preferred_e...  9.91 us
    all_gather x1, blocking collectives, local(): lax.all_gather(normed, 'head', axis=0, tiled=True)  7.94 us
    all_to_all x1, starting transfers between devices, local(): lax.all_to_all(outgoing, 'req', split_axis=0, concat_axis=0, tiled=True)  5.52 us
    dot_general x1, matrix products, local(): jnp.einsum('sjcd,jdf->sjcf', lax.all_to_all(outgoing, 'req', split_axis=0...  5.07 us
  transfers between devices with their start and end apart: 3, of which 3 were waited for; matrix products, arithmetic and copies ran while one was open for 3% of the time, Pallas kernels for 0%

commit v1 on v0

v1 whole, which is shorter than its diff:
```python
import functools

import jax
import jax.numpy as jnp
from jax import lax
from jax.experimental import pallas as pl
from jax.experimental.pallas import tpu as pltpu
from jax.sharding import PartitionSpec as P

D = 1536
HEADS = 24
KV = 8
HD = 64
F = 512
GROUP = HEADS // KV
LANES = 128
WIDE = D + LANES

EPSILON = 1e-06
THETA = 10000.0
MESH = pl.DeviceIdType.MESH
BF = jnp.bfloat16
F32 = jnp.float32


def rms_scale(wide, gain):
    mean_square = jnp.mean(wide * wide, axis=-1, keepdims=True)
    return (wide * lax.rsqrt(mean_square + EPSILON) * gain.astype(F32)).astype(BF)


class Axis:
    def __init__(self, name, A, B):
        self.name, self.A, self.B = name, A, B
        me = lax.axis_index(name)
        self.a, self.b = me // B, me % B

    def peers(self):
        A, B = self.A, self.B
        out = [((self.a + d) % A) * B + self.b for d in range(1, A)]
        return out + [self.a * B + (self.b + d) % B for d in range(1, B)]

    def copy(self, src, dst, send, recv, a, b):
        return pltpu.make_async_remote_copy(
            src_ref=src, dst_ref=dst, send_sem=send, recv_sem=recv,
            device_id={self.name: a * self.B + b}, device_id_type=MESH)


def gather_start(ax, buf, send, recv):
    sent = []
    a, b = ax.a, ax.b
    own = buf.at[a, b]
    for d in range(ax.A - 1, 0, -1):
        c = ax.copy(own, own, send.at[d, 0], recv.at[a, b], (a + d) % ax.A, b)
        c.start()
        sent.append(c)
    for d in range(1, ax.B):
        c = ax.copy(own, own, send.at[0, d], recv.at[a, b], a, (b + d) % ax.B)
        c.start()
        sent.append(c)
    return sent


def gather_forward(ax, buf, send, recv, sent):
    a, b = ax.a, ax.b
    for d in range(1, ax.A):
        o = (a + ax.A - d) % ax.A
        block = buf.at[o, b]
        ax.copy(block, block, send.at[0, 0], recv.at[o, b], a, b).wait_recv()
        for e in range(1, ax.B):
            c = ax.copy(block, block, send.at[d, e], recv.at[o, b], a, (b + e) % ax.B)
            c.start()
            sent.append(c)


def gather_column(ax, buf, send, recv, e):
    o = (ax.b + ax.B - e) % ax.B
    for d in range(ax.A):
        a = (ax.a + ax.A - d) % ax.A
        block = buf.at[a, o]
        ax.copy(block, block, send.at[0, 0], recv.at[a, o], ax.a, ax.b).wait_recv()
    return o


def scatter_minor(ax, part, rx, send, recv, e, sent):
    t = (ax.b + e) % ax.B
    for d in range(1, ax.A + 1):
        a = (ax.a + d) % ax.A
        c = ax.copy(part.at[a, t], rx.at[e - 1, a], send.at[e - 1, a], recv.at[e - 1, a], ax.a, t)
        c.start()
        sent.append(c)


def scatter_major(ax, part, rx, recv1, mid, rx2, send2, recv2, sent):
    a, b = ax.a, ax.b

    def column_sum(o):
        total = part[o, b].astype(F32)
        for e in range(1, ax.B):
            slot = rx.at[e - 1, o]
            ax.copy(slot, slot, send2.at[0], recv1.at[e - 1, o], a, b).wait_recv()
            total = total + rx[e - 1, o].astype(F32)
        return total

    for d in range(1, ax.A):
        o = (a + d) % ax.A
        mid[d - 1] = column_sum(o).astype(BF)
        c = ax.copy(mid.at[d - 1], rx2.at[d - 1], send2.at[d - 1], recv2.at[d - 1], o, b)
        c.start()
        sent.append(c)
    total = column_sum(a)
    for d in range(1, ax.A):
        slot = rx2.at[d - 1]
        ax.copy(slot, slot, send2.at[0], recv2.at[d - 1], a, b).wait_recv()
        total = total + rx2[d - 1].astype(F32)
    return total


def body(HA, HB, RA, RB, kvl, UN, NC,
         residual, gain1, wqkv_h, wout_h, cache_h, lengths, cos, sin, gain2, router, routes,
         win_h, wdown_h,
         out, newkv_out,
         wqkv, wout, cache, win, wdown,
         hbuf, rbuf, q8, nkv, o8, hpart, hrx, hmid, hrx2, rpart, rrx, rmid, rrx2, hid, lg,
         wsem, csem,
         hg_s, hg_r, hs_s, hs_r, hs2_s, hs2_r, rg_s, rg_r, rs_s, rs_r, rs2_s, rs2_r):
    T = residual.shape[0]
    R = cache.shape[0]
    E = router.shape[1]
    EL = win.shape[0]
    G = R * kvl // 2
    GC = G // NC
    head = Axis("head", HA, HB)
    req = Axis("req", RA, RB)
    parts = 1 if kvl == 2 else 2

    c_wqkv = pltpu.make_async_copy(wqkv_h, wqkv, wsem.at[0])
    c_wqkv.start()
    def cache_copy(c, s):
        rows = pl.ds(c * GC + s * G, GC)
        return pltpu.make_async_copy(cache_h.at[rows], cache.at[rows], csem.at[c, s])
    for c in range(NC):
        for s in range(parts):
            cache_copy(c, s).start()
    c_wout = pltpu.make_async_copy(wout_h, wout, wsem.at[1])
    c_wout.start()
    c_win = pltpu.make_async_copy(win_h, win, wsem.at[2])
    c_win.start()
    c_wdown = pltpu.make_async_copy(wdown_h, wdown, wsem.at[3])
    c_wdown.start()

    barrier = pltpu.get_barrier_semaphore()
    count = 0
    for ax in (head, req):
        for p in ax.peers():
            pl.semaphore_signal(barrier, inc=1, device_id={ax.name: p}, device_id_type=MESH)
            count += 1

    resid = residual[...].astype(F32)
    hbuf[head.a, head.b] = rms_scale(resid, gain1[...])
    pl.semaphore_wait(barrier, count)

    sent = gather_start(head, hbuf, hg_s, hg_r)
    q8[...] = jnp.zeros_like(q8)
    gather_forward(head, hbuf, hg_s, hg_r, sent)
    for e in range(1, HB):
        gather_column(head, hbuf, hg_s, hg_r, e)
    c_wqkv.wait()
    normed = hbuf[...].reshape(R, D)
    y = jnp.dot(normed, wqkv[...], preferred_element_type=F32)

    C = cos[...]
    S = sin[...]
    lane = lax.broadcasted_iota(jnp.int32, (R, LANES), 1)
    low = (lane & 32) == 0
    zero = jnp.zeros((R, HD), F32)

    def piece(i):
        return y[:, i * HD:(i + 1) * HD]

    def rot(x):
        swapped = jnp.where(low, pltpu.roll(x, LANES - 32, 1), pltpu.roll(x, 32, 1))
        return (x * C + swapped * S).astype(BF).astype(F32)

    for k in range(kvl):
        base = k * (GROUP + 2)
        for g in range(GROUP):
            x = rot(jnp.concatenate([piece(base + g), zero], axis=1)) * (HD ** -0.5)
            if kvl == 2:
                q8[k, pl.ds(k * GROUP + g, G, stride=8), :] = x
            else:
                q8[0, pl.ds(g, G, stride=8), :] = x[:G]
                q8[1, pl.ds(GROUP + g, G, stride=8), :] = x[G:]
        kv = jnp.concatenate([piece(base + GROUP), piece(base + GROUP + 1)], axis=1)
        kv = jnp.where(lane < HD, rot(kv), kv.astype(BF).astype(F32))
        nkv[:, k * LANES:(k + 1) * LANES] = kv
        newkv_out[:, k * LANES:(k + 1) * LANES] = kv.astype(BF)

    position = lax.broadcasted_iota(jnp.int32, (8, cache.shape[2]), 1)
    upper = lax.broadcasted_iota(jnp.int32, (8, cache.shape[2]), 0) >= GROUP

    def attend(first):
        ids = [first + u for u in range(UN)]
        rows8 = [pl.ds(pl.multiple_of(i * 8, 8), 8) for i in ids]
        qs = [jnp.concatenate([q8[0, r, :], q8[1, r, :]], axis=1) for r in rows8]
        if kvl == 2:
            kvs = [jnp.concatenate([cache[i, 0], cache[i, 1]], axis=1) for i in ids]
            nks = [nkv[pl.ds(i, 1), :] for i in ids]
            lens = [lengths[i] for i in ids]
        else:
            kvs = [jnp.concatenate([cache[i, 0], cache[i + G, 0]], axis=1) for i in ids]
            nks = [jnp.concatenate([nkv[pl.ds(i, 1), :], nkv[pl.ds(i + G, 1), :]], axis=1) for i in ids]
            lens = [jnp.where(upper, lengths[i + G], lengths[i]) for i in ids]
        ss = [lax.dot_general(q.astype(BF), kv, (((1,), (1,)), ((), ())), preferred_element_type=F32)
              for q, kv in zip(qs, kvs)]
        owns = [jnp.sum(q * nk, axis=1, keepdims=True) for q, nk in zip(qs, nks)]
        ms = [jnp.where(position < n, s, -1e30) for s, n in zip(ss, lens)]
        peaks = [jnp.maximum(jnp.max(m, axis=1, keepdims=True), o) for m, o in zip(ms, owns)]
        ws = [jnp.exp(m - p) for m, p in zip(ms, peaks)]
        ows = [jnp.exp(o - p) for o, p in zip(owns, peaks)]
        totals = [jnp.sum(w, axis=1, keepdims=True) + o for w, o in zip(ws, ows)]
        os = [jnp.dot(w.astype(BF), kv, preferred_element_type=F32) for w, kv in zip(ws, kvs)]
        for r, o, ow, nk, t in zip(rows8, os, ows, nks, totals):
            o = (o + ow.astype(BF).astype(F32) * nk) / t
            o8[0, r, :] = o[:, :LANES]
            o8[1, r, :] = o[:, LANES:]

    for c in range(NC):
        for s in range(parts):
            cache_copy(c, s).wait()

        @pl.loop(0, GC // UN)
        def _(step):
            attend(c * GC + step * UN)

    heads = []
    for k in range(kvl):
        for g in range(GROUP):
            if kvl == 2:
                z = o8[k, pl.ds(k * GROUP + g, G, stride=8), :]
            else:
                z = jnp.concatenate([o8[0, pl.ds(g, G, stride=8), :],
                                     o8[1, pl.ds(GROUP + g, G, stride=8), :]], axis=0)
            heads.append(z[:, HD:])
    attn = jnp.concatenate(heads, axis=1).astype(BF)
    c_wout.wait()
    attention = jnp.dot(attn, wout[...], preferred_element_type=F32).astype(BF)
    hpart[...] = attention.reshape(HA, HB, T, D)
    for e in range(1, HB):
        scatter_minor(head, hpart, hrx, hs_s, hs_r, e, sent)
    total = scatter_major(head, hpart, hrx, hs_r, hmid, hrx2, hs2_s, hs2_r, sent)
    attended = (resid + total).astype(BF).astype(F32)
    nm = rms_scale(attended, gain2[...])

    lg[...] = jnp.zeros_like(lg)
    lg[:, :E] = jnp.dot(nm, router[...], preferred_element_type=F32)
    logits = lg[...]
    tl = lax.broadcasted_iota(jnp.int32, (T, LANES), 1)
    hit = tl == routes[:, 0:1]
    for j in range(1, routes.shape[1]):
        hit = hit | (tl == routes[:, j:j + 1])
    top = jnp.max(jnp.where(hit, logits, -3e38), axis=1, keepdims=True)
    weight = jnp.where(hit, jnp.exp(jnp.where(hit, logits - top, 0.0)), 0.0)
    gates = weight / jnp.sum(weight, axis=1, keepdims=True)
    high = gates.astype(BF).astype(F32)
    gates = high + pltpu.roll(gates - high, HD, 1)
    rbuf[req.a, req.b, :, :D] = nm
    rbuf[req.a, req.b, :, D:] = gates.astype(BF)

    sent2 = gather_start(req, rbuf, rg_s, rg_r)
    gather_forward(req, rbuf, rg_s, rg_r, sent2)
    c_win.wait()
    c_wdown.wait()
    first = lax.axis_index("req") * EL
    M = RA * T

    def experts(col):
        x = rbuf[:, col, :, :D].reshape(M, D)
        gt = rbuf[:, col, :, D:].reshape(M, LANES).astype(F32)
        gt = gt + pltpu.roll(gt, HD, 1)
        glane = lax.broadcasted_iota(jnp.int32, (M, LANES), 1)

        def up(j, n):
            lo = n * 256
            gate_cols = jnp.dot(x, win[j, :, lo:lo + 256], preferred_element_type=F32)
            up_cols = jnp.dot(x, win[j, :, F + lo:F + lo + 256], preferred_element_type=F32)
            g = jnp.sum(jnp.where(glane == first + j, gt, 0.0), axis=1, keepdims=True)
            act = gate_cols / (1.0 + jnp.exp(-gate_cols)) * up_cols
            hid[j, :, lo:lo + 256] = (act * g).astype(BF)

        @pl.loop(0, EL)
        def _(j):
            for n in range(F // 256):
                up(j, n)

        for n in range(D // 512):
            acc = jnp.zeros((M, 512), F32)
            for j in range(EL):
                acc = acc + jnp.dot(hid[j], wdown[j, :, n * 512:(n + 1) * 512],
                                    preferred_element_type=F32)
            rpart[:, col, :, n * 512:(n + 1) * 512] = acc.astype(BF).reshape(RA, T, 512)

    experts(req.b)
    for e in range(1, RB):
        o = gather_column(req, rbuf, rg_s, rg_r, e)
        experts(o)
        scatter_minor(req, rpart, rrx, rs_s, rs_r, RB - e, sent2)
    mixed = scatter_major(req, rpart, rrx, rs_r, rmid, rrx2, rs2_s, rs2_r, sent2)
    out[...] = (attended + mixed).astype(BF)
    for c in sent + sent2:
        c.wait_send()


def local(head_n, req_n, residual_in, attn_gain, w_qkv, w_out, kv_cache, lengths,
          moe_gain, w_router, routes, w_in, w_down):
    T = residual_in.shape[0]
    R, kvl, L = kv_cache.shape[:3]
    E = w_router.shape[1]
    EL = w_in.shape[0]
    HB = 2 if head_n % 2 == 0 else 1
    HA = head_n // HB
    RA = 4 if req_n % 4 == 0 else 1
    RB = req_n // RA
    G = R * kvl // 2
    UN, NC = 8, 4
    index = jnp.arange(HD // 2).astype(F32)
    frequency = jnp.power(THETA, -2.0 * index / HD)
    angle = lengths.astype(F32)[:, None] * frequency[None, :]
    c, s = jnp.cos(angle), jnp.sin(angle)
    cos = jnp.concatenate([c, c, c, c], axis=1)
    sin = jnp.concatenate([-s, s, -s, s], axis=1)
    vm = pl.BlockSpec(memory_space=pltpu.VMEM)
    sm = pl.BlockSpec(memory_space=pltpu.SMEM)
    hbm = pl.BlockSpec(memory_space=pl.ANY)
    dma = pltpu.SemaphoreType.DMA
    V = pltpu.VMEM
    mn = lambda n: max(n, 1)
    layer_out, new_kv = pl.pallas_call(
        functools.partial(body, HA, HB, RA, RB, kvl, UN, NC),
        out_shape=(jax.ShapeDtypeStruct((T, D), BF),
                   jax.ShapeDtypeStruct((R, kvl * LANES), BF)),
        in_specs=[vm, vm, hbm, hbm, hbm, sm, vm, vm, vm, vm, vm, hbm, hbm],
        out_specs=(vm, vm),
        scratch_shapes=[
            V((D, kvl * (GROUP + 2) * HD), BF), V(w_out.shape, BF), V(kv_cache.shape, BF),
            V(w_in.shape, BF), V(w_down.shape, BF),
            V((HA, HB, T, D), BF), V((RA, RB, T, WIDE), BF),
            V((2, G * 8, LANES), F32), V((R, kvl * LANES), F32), V((2, G * 8, LANES), F32),
            V((HA, HB, T, D), BF), V((mn(HB - 1), HA, T, D), BF),
            V((mn(HA - 1), T, D), BF), V((mn(HA - 1), T, D), BF),
            V((RA, RB, T, D), BF), V((mn(RB - 1), RA, T, D), BF),
            V((mn(RA - 1), T, D), BF), V((mn(RA - 1), T, D), BF),
            V((EL, RA * T, F), BF), V((T, LANES), F32),
            dma((4,)), dma((NC, 2)),
            dma((HA, HB)), dma((HA, HB)), dma((mn(HB - 1), HA)), dma((mn(HB - 1), HA)),
            dma((mn(HA - 1),)), dma((mn(HA - 1),)),
            dma((RA, RB)), dma((RA, RB)), dma((mn(RB - 1), RA)), dma((mn(RB - 1), RA)),
            dma((mn(RA - 1),)), dma((mn(RA - 1),)),
        ],
        compiler_params=pltpu.CompilerParams(
            collective_id=0, has_side_effects=True, vmem_limit_bytes=56 << 20),
        name="layer",
    )(residual_in, attn_gain.reshape(1, D), w_qkv.reshape(D, kvl * (GROUP + 2) * HD), w_out,
      kv_cache, lengths, cos, sin, moe_gain.reshape(1, D), w_router, routes, w_in, w_down)
    return layer_out, new_kv.reshape(R, kvl, LANES)


def solution(mesh):
    return jax.shard_map(
        functools.partial(local, mesh.shape["head"], mesh.shape["req"]),
        mesh=mesh,
        in_specs=(
            P(("req", "head"), None),
            P(),
            P(None, "head", None),
            P("head", None),
            P("req", "head", None, None),
            P("req"),
            P(),
            P(),
            P(("req", "head"), None),
            P("req", None, None),
            P("req", None, None),
        ),
        out_specs=(P(("req", "head"), None), P("req", "head", None)),
        check_vma=False,
    )
```

time: 165 us -> 72.7 us (0.44)
  waiting for transfers between devices: 73.8 us -> 0 us
  Pallas kernels: 0 us -> 57 us
  matrix products: 32.6 us -> 0 us
  between operations: 14.3 us -> 0.65 us
  starting transfers between devices: 9.81 us -> 0 us
  other arithmetic: 11.2 us -> 1.8 us
  blocking collectives: 7.94 us -> 0 us
    pallas_call x0 -> x1, Pallas kernels: none -> 57 us  [local(): pl.pallas_call(functools.partial(body, HA, HB, RA, RB, kvl, UN, NC), out_...]
    all_to_all x2 -> x0, waiting for transfers between devices: 53.1 us -> none  [the longest x1 28.4 us: local(): lax.all_to_all(outgoing, 'req', split_axis=0, concat_axis=0, tiled=True)]
    dot_general x8 -> x0, matrix products: 32.6 us -> none  [the longest x1 12 us: attend_full(): jnp.einsum('rkgd,rkld->rkgl', queries, cache[..., :HD], preferred_element...]
    reduce_scatter x1 -> x0, waiting for transfers between devices: 20.7 us -> none  [local(): lax.psum_scatter(jnp.dot(attn_heads, w_out, preferred_element_type=jnp.fl...]
    all_to_all x2 -> x0, starting transfers between devices: 9.77 us -> none  [the longest x1 5.52 us: local(): lax.all_to_all(outgoing, 'req', split_axis=0, concat_axis=0, tiled=True)]
    all_gather x1 -> x0, blocking collectives: 7.94 us -> none  [local(): lax.all_gather(normed, 'head', axis=0, tiled=True)]
    reshape x3 -> x4, local copies, waits for them, and re-layouts: 2.63 us -> 8.09 us  [the longest x1 4.02 us: local(): w_qkv.reshape(D, kvl * (GROUP + 2) * HD)]
    reduce_sum x7 -> x0, other arithmetic: 5.19 us -> none  [the longest x2 2.05 us: rms_scale(): mean_square = jnp.mean(wide * wide, axis=-1, keepdims=True)]
  transfers between devices with their start and end apart: 3 -> 0, of which waited for: 3 -> 0; matrix products, arithmetic and copies ran while one was open for 3% -> 0% of each run, Pallas kernels for 0% -> 0%
where the time goes in v1:
time: 72.7 us; the launch traced here: 72.3 us
  Pallas kernels  57 us (78%)
  local copies, waits for them, and re-layouts  12.8 us (18%)
  other arithmetic  1.8 us (2%)
    pallas_call x1, Pallas kernels, local(): pl.pallas_call(functools.partial(body, HA, HB, RA, RB, kvl, UN, NC), out_...  57 us
    unnamed x3, local copies, waits for them, and re-layouts  4.73 us
    reshape x1, local copies, waits for them, and re-layouts, local(): w_qkv.reshape(D, kvl * (GROUP + 2) * HD)  4.02 us
    reshape x1, local copies, waits for them, and re-layouts, local(): return (layer_out, new_kv.reshape(R, kvl, LANES))  1.49 us

profile of v1, /device:TPU:0, one launch (start us, length us, event | category | flops | bytes accessed | tf_op | source)
XLA Modules:
  0.0 72.3 jit_solution(7073883791248206826)
XLA Ops:
  0.6 0.7 convert_element_type.10
  1.3 1.3 %reshape.23.gain1 = bf16[1,1536]{1,0:T(2,128)(2,1)} reshape(bf16[1536]{0:T(1024)(128)(2,1)} %param.12) | data formatting | bytes 6144 | tf_op jit(solution)/shard_map/reshape | solution.py:362
  2.6 1.3 %reshape.25.gain2 = bf16[1,1536]{1,0:T(2,128)(2,1)} reshape(bf16[1536]{0:T(1024)(128)(2,1)} %param.17) | data formatting | bytes 6144 | tf_op jit(solution)/shard_map/reshape | solution.py:363
  3.9 1.4 %copy.22.routes = s32[32,8]{1,0:T(8,128)} copy(s32[32,8]{0,1:T(8,128)} %param.19) | data formatting | bytes 2048 | tf_op args[8]
  5.2 0.3 fusion
  5.5 0.8 %pad_maximum_fusion = (f32[128,128]{1,0:T(8,128)}, f32[128,128]{1,0:T(8,128)}) fusion(f32[128,32]{1,0:T(8,128)S(1)} %get-tuple-element.8, f32[128,32]{1,0:T(8,128)S(1)} %get-tuple-element.7, f32[128,32]{1,0:T(8,128)S(1)} %get-tuple-element.6), kind=kLoop, calls=%fused_computation.2 | loop fusion | flops 98304 | bytes 180224 | tf_op jit(solution)/shard_map/concatenate | solution.py:329
  6.4 1.8 %copy.21.router = bf16[1536,24]{1,0:T(8,128)(2,1)} copy(bf16[1536,24]{0,1:T(8,128)(2,1)} %param.18) | data formatting | bytes 147456 | tf_op args[7]
  8.2 4.0 %copy.20.wqkv_h = bf16[1536,640]{1,0:T(8,128)(2,1)} copy(bf16[1536,640]{0,1:T(8,128)(2,1)} %bitcast.1) | data formatting | bytes 3932160 | tf_op jit(solution)/shard_map/reshape | solution.py:362
  12.2 57.0 %layer.1 = (bf16[32,1536]{1,0:T(8,128)(2,1)}, bf16[128,256]{1,0:T(8,128)(2,1)}) custom-call(bf16[32,1536]{1,0:T(8,128)(2,1)} %residual.1, bf16[1,1536]{1,0:T(2,128)(2,1)} %reshape.23.gain1, bf16[1536,640]{1,0:T(8,128)(2,1)} %copy.20.wqkv_h, bf16[384,1536]{1,0:T(8,128)(2,1)} %wout_h.1, bf16[128,2,192,128]{3,2,1,0:T(8,128)(2,1)} %cache_h.1, s32[128]{0:T(128)} %lengths.1, ...), custom_call_target="tpu_custom_call" | custom-call | tf_op jit(solution)/shard_map/layer/pallas_call | solution.py:337
  69.3 1.5 %reshape.26 = bf16[128,2,128]{2,1,0:T(2,128)(2,1)} reshape(bf16[128,256]{1,0:T(8,128)(2,1)} %get-tuple-element.5) | data formatting | bytes 131072 | tf_op jit(solution)/shard_map/reshape | solution.py:364
  70.8 1.5 %copy.24 = bf16[32,1536]{1,0:T(8,128)(2,1)} copy(bf16[32,1536]{1,0:T(8,128)(2,1)} %get-tuple-element.13) | data formatting | bytes 196608
  (1 shorter events, 0.0 us)

commit v2 on v1

--- a/solution.py
+++ b/solution.py
@@ -2,6 +2,7 @@
 
 import jax
 import jax.numpy as jnp
+import numpy as np
 from jax import lax
 from jax.experimental import pallas as pl
 from jax.experimental.pallas import tpu as pltpu
@@ -18,6 +19,7 @@
 
 EPSILON = 1e-06
 THETA = 10000.0
+CHUNKS = 2
 MESH = pl.DeviceIdType.MESH
 BF = jnp.bfloat16
 F32 = jnp.float32
@@ -26,6 +28,20 @@
 def rms_scale(wide, gain):
     mean_square = jnp.mean(wide * wide, axis=-1, keepdims=True)
     return (wide * lax.rsqrt(mean_square + EPSILON) * gain.astype(F32)).astype(BF)
+
+
+def row(ref):
+    wide = ref[...].astype(F32)
+    return jnp.concatenate([wide[i:i + 1] for i in range(wide.shape[0])], axis=1)
+
+
+def dot_nt(a, b):
+    return lax.dot_general(a, b, (((1,), (1,)), ((), ())), preferred_element_type=F32)
+
+
+def eye(n):
+    same = lax.broadcasted_iota(jnp.int32, (n, n), 0) == lax.broadcasted_iota(jnp.int32, (n, n), 1)
+    return jnp.where(same, 1.0, 0.0).astype(BF)
 
 
 class Axis:
@@ -45,18 +61,22 @@
             device_id={self.name: a * self.B + b}, device_id_type=MESH)
 
 
+def chunk(buf, o, p, c):
+    rows = buf.shape[2] // CHUNKS
+    return buf.at[o, p, pl.ds(c * rows, rows)]
+
+
 def gather_start(ax, buf, send, recv):
     sent = []
     a, b = ax.a, ax.b
-    own = buf.at[a, b]
-    for d in range(ax.A - 1, 0, -1):
-        c = ax.copy(own, own, send.at[d, 0], recv.at[a, b], (a + d) % ax.A, b)
-        c.start()
-        sent.append(c)
-    for d in range(1, ax.B):
-        c = ax.copy(own, own, send.at[0, d], recv.at[a, b], a, (b + d) % ax.B)
-        c.start()
-        sent.append(c)
+    for c in range(CHUNKS):
+        own = chunk(buf, a, b, c)
+        if ax.A > 1:
+            sent.append(ax.copy(own, own, send.at[0, 0, c], recv.at[a, b, c], (a + 1) % ax.A, b))
+            sent[-1].start()
+        for d in range(1, ax.B):
+            sent.append(ax.copy(own, own, send.at[0, d, c], recv.at[a, b, c], a, (b + d) % ax.B))
+            sent[-1].start()
     return sent
 
 
@@ -64,20 +84,26 @@
     a, b = ax.a, ax.b
     for d in range(1, ax.A):
         o = (a + ax.A - d) % ax.A
-        block = buf.at[o, b]
-        ax.copy(block, block, send.at[0, 0], recv.at[o, b], a, b).wait_recv()
-        for e in range(1, ax.B):
-            c = ax.copy(block, block, send.at[d, e], recv.at[o, b], a, (b + e) % ax.B)
-            c.start()
-            sent.append(c)
+        for c in range(CHUNKS):
+            block = chunk(buf, o, b, c)
+            ax.copy(block, block, send.at[0, 0, c], recv.at[o, b, c], a, b).wait_recv()
+            if d < ax.A - 1:
+                sent.append(ax.copy(block, block, send.at[d, 0, c], recv.at[o, b, c],
+                                    (a + 1) % ax.A, b))
+                sent[-1].start()
+            for e in range(1, ax.B):
+                sent.append(ax.copy(block, block, send.at[d, e, c], recv.at[o, b, c],
+                                    a, (b + e) % ax.B))
+                sent[-1].start()
 
 
 def gather_column(ax, buf, send, recv, e):
     o = (ax.b + ax.B - e) % ax.B
     for d in range(ax.A):
         a = (ax.a + ax.A - d) % ax.A
-        block = buf.at[a, o]
-        ax.copy(block, block, send.at[0, 0], recv.at[a, o], ax.a, ax.b).wait_recv()
+        for c in range(CHUNKS):
+            block = chunk(buf, a, o, c)
+            ax.copy(block, block, send.at[0, 0, c], recv.at[a, o, c], ax.a, ax.b).wait_recv()
     return o
 
 
@@ -116,16 +142,16 @@
 
 
 def body(HA, HB, RA, RB, kvl, UN, NC,
-         residual, gain1, wqkv_h, wout_h, cache_h, lengths, cos, sin, gain2, router, routes,
+         residual, gain1, wqkv_h, wout_h, cache_h, lengths, lenrow, freq, gain2, router, routes,
          win_h, wdown_h,
          out, newkv_out,
          wqkv, wout, cache, win, wdown,
-         hbuf, rbuf, q8, nkv, o8, hpart, hrx, hmid, hrx2, rpart, rrx, rmid, rrx2, hid, lg,
+         hbuf, rbuf, q8, nkv, o8, hpart, hrx, hmid, hrx2, rpart, rrx, rmid, rrx2, hid, lg, hits,
          wsem, csem,
          hg_s, hg_r, hs_s, hs_r, hs2_s, hs2_r, rg_s, rg_r, rs_s, rs_r, rs2_s, rs2_r):
     T = residual.shape[0]
     R = cache.shape[0]
-    E = router.shape[1]
+    E = router.shape[0]
     EL = win.shape[0]
     G = R * kvl // 2
     GC = G // NC
@@ -156,22 +182,30 @@
             count += 1
 
     resid = residual[...].astype(F32)
-    hbuf[head.a, head.b] = rms_scale(resid, gain1[...])
+    hbuf[head.a, head.b] = rms_scale(resid, row(gain1))
     pl.semaphore_wait(barrier, count)
 
     sent = gather_start(head, hbuf, hg_s, hg_r)
     q8[...] = jnp.zeros_like(q8)
+    lane = lax.broadcasted_iota(jnp.int32, (R, LANES), 1)
+    low = (lane & 32) == 0
+    column = dot_nt(eye(R), jnp.broadcast_to(lenrow[...].astype(F32), (LANES, R)).astype(BF))
+    angle = column * freq[...]
+    C = jnp.cos(angle)
+    S = jnp.sin(angle)
+    S = jnp.where(low, -S, S)
+    expert = lax.broadcasted_iota(jnp.int32, (LANES, T), 0)
+    hit = expert == routes[0:1, :]
+    for j in range(1, routes.shape[0]):
+        hit = hit | (expert == routes[j:j + 1, :])
+    hits[...] = dot_nt(eye(T), jnp.where(hit, 1.0, 0.0).astype(BF))
     gather_forward(head, hbuf, hg_s, hg_r, sent)
     for e in range(1, HB):
         gather_column(head, hbuf, hg_s, hg_r, e)
     c_wqkv.wait()
     normed = hbuf[...].reshape(R, D)
-    y = jnp.dot(normed, wqkv[...], preferred_element_type=F32)
-
-    C = cos[...]
-    S = sin[...]
-    lane = lax.broadcasted_iota(jnp.int32, (R, LANES), 1)
-    low = (lane & 32) == 0
+    y = dot_nt(normed, wqkv[...])
+
     zero = jnp.zeros((R, HD), F32)
 
     def piece(i):
@@ -193,7 +227,7 @@
         kv = jnp.concatenate([piece(base + GROUP), piece(base + GROUP + 1)], axis=1)
         kv = jnp.where(lane < HD, rot(kv), kv.astype(BF).astype(F32))
         nkv[:, k * LANES:(k + 1) * LANES] = kv
-        newkv_out[:, k * LANES:(k + 1) * LANES] = kv.astype(BF)
+        newkv_out[:, k, :] = kv.astype(BF)
 
     position = lax.broadcasted_iota(jnp.int32, (8, cache.shape[2]), 1)
     upper = lax.broadcasted_iota(jnp.int32, (8, cache.shape[2]), 0) >= GROUP
@@ -210,8 +244,7 @@
             kvs = [jnp.concatenate([cache[i, 0], cache[i + G, 0]], axis=1) for i in ids]
             nks = [jnp.concatenate([nkv[pl.ds(i, 1), :], nkv[pl.ds(i + G, 1), :]], axis=1) for i in ids]
             lens = [jnp.where(upper, lengths[i + G], lengths[i]) for i in ids]
-        ss = [lax.dot_general(q.astype(BF), kv, (((1,), (1,)), ((), ())), preferred_element_type=F32)
-              for q, kv in zip(qs, kvs)]
+        ss = [dot_nt(q.astype(BF), kv) for q, kv in zip(qs, kvs)]
         owns = [jnp.sum(q * nk, axis=1, keepdims=True) for q, nk in zip(qs, nks)]
         ms = [jnp.where(position < n, s, -1e30) for s, n in zip(ss, lens)]
         peaks = [jnp.maximum(jnp.max(m, axis=1, keepdims=True), o) for m, o in zip(ms, owns)]
@@ -249,15 +282,12 @@
         scatter_minor(head, hpart, hrx, hs_s, hs_r, e, sent)
     total = scatter_major(head, hpart, hrx, hs_r, hmid, hrx2, hs2_s, hs2_r, sent)
     attended = (resid + total).astype(BF).astype(F32)
-    nm = rms_scale(attended, gain2[...])
+    nm = rms_scale(attended, row(gain2))
 
     lg[...] = jnp.zeros_like(lg)
-    lg[:, :E] = jnp.dot(nm, router[...], preferred_element_type=F32)
+    lg[:, :E] = dot_nt(nm, router[...])
     logits = lg[...]
-    tl = lax.broadcasted_iota(jnp.int32, (T, LANES), 1)
-    hit = tl == routes[:, 0:1]
-    for j in range(1, routes.shape[1]):
-        hit = hit | (tl == routes[:, j:j + 1])
+    hit = hits[...] > 0.5
     top = jnp.max(jnp.where(hit, logits, -3e38), axis=1, keepdims=True)
     weight = jnp.where(hit, jnp.exp(jnp.where(hit, logits - top, 0.0)), 0.0)
     gates = weight / jnp.sum(weight, axis=1, keepdims=True)
@@ -308,6 +338,11 @@
     out[...] = (attended + mixed).astype(BF)
     for c in sent + sent2:
         c.wait_send()
+
+
+def pinned(*arrays):
+    return [a if i == 5 else pltpu.with_memory_space_constraint(a, pltpu.HBM)
+            for i, a in enumerate(arrays)]
 
 
 def local(head_n, req_n, residual_in, attn_gain, w_qkv, w_out, kv_cache, lengths,
@@ -322,26 +357,23 @@
     RB = req_n // RA
     G = R * kvl // 2
     UN, NC = 8, 4
-    index = jnp.arange(HD // 2).astype(F32)
-    frequency = jnp.power(THETA, -2.0 * index / HD)
-    angle = lengths.astype(F32)[:, None] * frequency[None, :]
-    c, s = jnp.cos(angle), jnp.sin(angle)
-    cos = jnp.concatenate([c, c, c, c], axis=1)
-    sin = jnp.concatenate([-s, s, -s, s], axis=1)
+    index = np.arange(HD // 2)
+    freq = np.power(THETA, -2.0 * index / HD).astype(np.float32)
+    freq = np.tile(freq, 4).reshape(1, LANES)
     vm = pl.BlockSpec(memory_space=pltpu.VMEM)
     sm = pl.BlockSpec(memory_space=pltpu.SMEM)
-    hbm = pl.BlockSpec(memory_space=pl.ANY)
+    hbm = pl.BlockSpec(memory_space=pltpu.HBM)
     dma = pltpu.SemaphoreType.DMA
     V = pltpu.VMEM
     mn = lambda n: max(n, 1)
     layer_out, new_kv = pl.pallas_call(
         functools.partial(body, HA, HB, RA, RB, kvl, UN, NC),
         out_shape=(jax.ShapeDtypeStruct((T, D), BF),
-                   jax.ShapeDtypeStruct((R, kvl * LANES), BF)),
+                   jax.ShapeDtypeStruct((R, kvl, LANES), BF)),
         in_specs=[vm, vm, hbm, hbm, hbm, sm, vm, vm, vm, vm, vm, hbm, hbm],
         out_specs=(vm, vm),
         scratch_shapes=[
-            V((D, kvl * (GROUP + 2) * HD), BF), V(w_out.shape, BF), V(kv_cache.shape, BF),
+            V((kvl * (GROUP + 2) * HD, D), BF), V(w_out.shape, BF), V(kv_cache.shape, BF),
             V(w_in.shape, BF), V(w_down.shape, BF),
             V((HA, HB, T, D), BF), V((RA, RB, T, WIDE), BF),
             V((2, G * 8, LANES), F32), V((R, kvl * LANES), F32), V((2, G * 8, LANES), F32),
@@ -349,19 +381,21 @@
             V((mn(HA - 1), T, D), BF), V((mn(HA - 1), T, D), BF),
             V((RA, RB, T, D), BF), V((mn(RB - 1), RA, T, D), BF),
             V((mn(RA - 1), T, D), BF), V((mn(RA - 1), T, D), BF),
-            V((EL, RA * T, F), BF), V((T, LANES), F32),
+            V((EL, RA * T, F), BF), V((T, LANES), F32), V((T, LANES), F32),
             dma((4,)), dma((NC, 2)),
-            dma((HA, HB)), dma((HA, HB)), dma((mn(HB - 1), HA)), dma((mn(HB - 1), HA)),
+            dma((HA, HB, CHUNKS)), dma((HA, HB, CHUNKS)), dma((mn(HB - 1), HA)), dma((mn(HB - 1), HA)),
             dma((mn(HA - 1),)), dma((mn(HA - 1),)),
-            dma((RA, RB)), dma((RA, RB)), dma((mn(RB - 1), RA)), dma((mn(RB - 1), RA)),
+            dma((RA, RB, CHUNKS)), dma((RA, RB, CHUNKS)), dma((mn(RB - 1), RA)), dma((mn(RB - 1), RA)),
             dma((mn(RA - 1),)), dma((mn(RA - 1),)),
         ],
         compiler_params=pltpu.CompilerParams(
-            collective_id=0, has_side_effects=True, vmem_limit_bytes=56 << 20),
+            collective_id=0, has_side_effects=True, vmem_limit_bytes=44 << 20),
         name="layer",
-    )(residual_in, attn_gain.reshape(1, D), w_qkv.reshape(D, kvl * (GROUP + 2) * HD), w_out,
-      kv_cache, lengths, cos, sin, moe_gain.reshape(1, D), w_router, routes, w_in, w_down)
-    return layer_out, new_kv.reshape(R, kvl, LANES)
+    )(*pinned(residual_in, attn_gain.reshape(D // LANES, LANES),
+      w_qkv.transpose(1, 2, 0).reshape(kvl * (GROUP + 2) * HD, D), w_out,
+      kv_cache, lengths, lengths.reshape(1, R), freq, moe_gain.reshape(D // LANES, LANES),
+      w_router.T, routes.T, w_in, w_down))
+    return layer_out, new_kv
 
 
 def solution(mesh):

time: 72.7 us -> 56.3 us (0.77)
  local copies, waits for them, and re-layouts: 12.8 us -> 1.27 us
  Pallas kernels: 57 us -> 54.2 us
  other arithmetic: 1.8 us -> 0 us
    reshape x4 -> x0, local copies, waits for them, and re-layouts: 8.09 us -> none  [the longest x1 4.02 us: local(): w_qkv.reshape(D, kvl * (GROUP + 2) * HD)]
    unnamed x3 -> x2, local copies, waits for them, and re-layouts: 4.73 us -> 1.27 us
    pallas_call x1, Pallas kernels: 57 us -> 54.2 us  [local(): pl.pallas_call(functools.partial(body, HA, HB, RA, RB, kvl, UN, NC), out_...]
    concatenate x1 -> x0, other arithmetic: 0.83 us -> none  [local(): cos = jnp.concatenate([c, c, c, c], axis=1)]
where the time goes in v2:
time: 56.3 us; the launch traced here: 56.1 us
  Pallas kernels  54.2 us (96%)
  local copies, waits for them, and re-layouts  1.27 us (2%)
  between operations  0.64 us (1%)
    pallas_call x1, Pallas kernels, local(): pl.pallas_call(functools.partial(body, HA, HB, RA, RB, kvl, UN, NC), out_...  54.2 us
    unnamed x2, local copies, waits for them, and re-layouts  1.27 us

profile of v2, /device:TPU:0, one launch (start us, length us, event | category | flops | bytes accessed | tf_op | source)
XLA Modules:
  0.0 56.1 jit_solution(5627010246393630157)
XLA Ops:
  0.6 54.2 %layer.1 = (bf16[32,1536]{1,0:T(8,128)(2,1)S(1)}, bf16[128,2,128]{2,1,0:T(2,128)(2,1)S(1)}) custom-call(bf16[32,1536]{1,0:T(8,128)(2,1)} %residual.1, bf16[12,128]{1,0:T(8,128)(2,1)} %bitcast.10, bf16[640,1536]{1,0:T(8,128)(2,1)} %bitcast.8, bf16[384,1536]{1,0:T(8,128)(2,1)} %wout_h.1, bf16[128,2,192,128]{3,2,1,0:T(8,128)(2,1)} %cache_h.1, s32[128]{0:T(128)} %lengths.1, ...), custom_call_target="tpu_custom_call" | custom-call | tf_op jit(solution)/shard_map/layer/pallas_call | solution.py:369
  54.9 0.6 %copy.16 = bf16[32,1536]{1,0:T(8,128)(2,1)} copy(bf16[32,1536]{1,0:T(8,128)(2,1)S(1)} %get-tuple-element.4) | data formatting | bytes 196608
  55.5 0.6 %copy.17 = bf16[128,2,128]{2,1,0:T(2,128)(2,1)} copy(bf16[128,2,128]{2,1,0:T(2,128)(2,1)S(1)} %get-tuple-element.5) | data formatting | bytes 131072

commit v3 on v2

--- a/solution.py
+++ b/solution.py
@@ -109,36 +109,44 @@
 
 def scatter_minor(ax, part, rx, send, recv, e, sent):
     t = (ax.b + e) % ax.B
+    rows = part.shape[2] // CHUNKS
     for d in range(1, ax.A + 1):
         a = (ax.a + d) % ax.A
-        c = ax.copy(part.at[a, t], rx.at[e - 1, a], send.at[e - 1, a], recv.at[e - 1, a], ax.a, t)
-        c.start()
-        sent.append(c)
+        for c in range(CHUNKS):
+            sent.append(ax.copy(chunk(part, a, t, c), rx.at[e - 1, a, pl.ds(c * rows, rows)],
+                                send.at[e - 1, a, c], recv.at[e - 1, a, c], ax.a, t))
+            sent[-1].start()
 
 
 def scatter_major(ax, part, rx, recv1, mid, rx2, send2, recv2, sent):
     a, b = ax.a, ax.b
-
-    def column_sum(o):
-        total = part[o, b].astype(F32)
+    rows = part.shape[2] // CHUNKS
+
+    def column_sum(o, c):
+        span = pl.ds(c * rows, rows)
+        total = part[o, b, span].astype(F32)
         for e in range(1, ax.B):
-            slot = rx.at[e - 1, o]
-            ax.copy(slot, slot, send2.at[0], recv1.at[e - 1, o], a, b).wait_recv()
-            total = total + rx[e - 1, o].astype(F32)
+            slot = rx.at[e - 1, o, span]
+            ax.copy(slot, slot, send2.at[0, 0], recv1.at[e - 1, o, c], a, b).wait_recv()
+            total = total + rx[e - 1, o, span].astype(F32)
         return total
 
     for d in range(1, ax.A):
         o = (a + d) % ax.A
-        mid[d - 1] = column_sum(o).astype(BF)
-        c = ax.copy(mid.at[d - 1], rx2.at[d - 1], send2.at[d - 1], recv2.at[d - 1], o, b)
-        c.start()
-        sent.append(c)
-    total = column_sum(a)
+        for c in range(CHUNKS):
+            span = pl.ds(c * rows, rows)
+            mid[d - 1, span] = column_sum(o, c).astype(BF)
+            sent.append(ax.copy(mid.at[d - 1, span], rx2.at[d - 1, span],
+                                send2.at[d - 1, c], recv2.at[d - 1, c], o, b))
+            sent[-1].start()
+    totals = [column_sum(a, c) for c in range(CHUNKS)]
     for d in range(1, ax.A):
-        slot = rx2.at[d - 1]
-        ax.copy(slot, slot, send2.at[0], recv2.at[d - 1], a, b).wait_recv()
-        total = total + rx2[d - 1].astype(F32)
-    return total
+        for c in range(CHUNKS):
+            span = pl.ds(c * rows, rows)
+            slot = rx2.at[d - 1, span]
+            ax.copy(slot, slot, send2.at[0, 0], recv2.at[d - 1, c], a, b).wait_recv()
+            totals[c] = totals[c] + rx2[d - 1, span].astype(F32)
+    return jnp.concatenate(totals, axis=0)
 
 
 def body(HA, HB, RA, RB, kvl, UN, NC,
@@ -356,7 +364,7 @@
     RA = 4 if req_n % 4 == 0 else 1
     RB = req_n // RA
     G = R * kvl // 2
-    UN, NC = 8, 4
+    UN, NC = 16, 4
     index = np.arange(HD // 2)
     freq = np.power(THETA, -2.0 * index / HD).astype(np.float32)
     freq = np.tile(freq, 4).reshape(1, LANES)
@@ -383,10 +391,10 @@
             V((mn(RA - 1), T, D), BF), V((mn(RA - 1), T, D), BF),
             V((EL, RA * T, F), BF), V((T, LANES), F32), V((T, LANES), F32),
             dma((4,)), dma((NC, 2)),
-            dma((HA, HB, CHUNKS)), dma((HA, HB, CHUNKS)), dma((mn(HB - 1), HA)), dma((mn(HB - 1), HA)),
-            dma((mn(HA - 1),)), dma((mn(HA - 1),)),
-            dma((RA, RB, CHUNKS)), dma((RA, RB, CHUNKS)), dma((mn(RB - 1), RA)), dma((mn(RB - 1), RA)),
-            dma((mn(RA - 1),)), dma((mn(RA - 1),)),
+            dma((HA, HB, CHUNKS)), dma((HA, HB, CHUNKS)), dma((mn(HB - 1), HA, CHUNKS)), dma((mn(HB - 1), HA, CHUNKS)),
+            dma((mn(HA - 1), CHUNKS)), dma((mn(HA - 1), CHUNKS)),
+            dma((RA, RB, CHUNKS)), dma((RA, RB, CHUNKS)), dma((mn(RB - 1), RA, CHUNKS)), dma((mn(RB - 1), RA, CHUNKS)),
+            dma((mn(RA - 1), CHUNKS)), dma((mn(RA - 1), CHUNKS)),
         ],
         compiler_params=pltpu.CompilerParams(
             collective_id=0, has_side_effects=True, vmem_limit_bytes=44 << 20),

time: 56.3 us -> 53.4 us (0.948)
  Pallas kernels: 54.2 us -> 51.3 us
    pallas_call x1, Pallas kernels: 54.2 us -> 51.3 us  [local(): pl.pallas_call(functools.partial(body, HA, HB, RA, RB, kvl, UN, NC), out_...]
where the time goes in v3:
time: 53.4 us; the launch traced here: 53.2 us
  Pallas kernels  51.3 us (96%)
  local copies, waits for them, and re-layouts  1.27 us (2%)
  between operations  0.64 us (1%)
    pallas_call x1, Pallas kernels, local(): pl.pallas_call(functools.partial(body, HA, HB, RA, RB, kvl, UN, NC), out_...  51.3 us
    unnamed x2, local copies, waits for them, and re-layouts  1.27 us

profile of v3, /device:TPU:0, one launch (start us, length us, event | category | flops | bytes accessed | tf_op | source)
XLA Modules:
  0.0 53.2 jit_solution(11139787358609098008)
XLA Ops:
  0.6 51.3 %layer.1 = (bf16[32,1536]{1,0:T(8,128)(2,1)S(1)}, bf16[128,2,128]{2,1,0:T(2,128)(2,1)S(1)}) custom-call(bf16[32,1536]{1,0:T(8,128)(2,1)} %residual.1, bf16[12,128]{1,0:T(8,128)(2,1)} %bitcast.10, bf16[640,1536]{1,0:T(8,128)(2,1)} %bitcast.8, bf16[384,1536]{1,0:T(8,128)(2,1)} %wout_h.1, bf16[128,2,192,128]{3,2,1,0:T(8,128)(2,1)} %cache_h.1, s32[128]{0:T(128)} %lengths.1, ...), custom_call_target="tpu_custom_call" | custom-call | tf_op jit(solution)/shard_map/layer/pallas_call | solution.py:377
  51.9 0.6 %copy.16 = bf16[32,1536]{1,0:T(8,128)(2,1)} copy(bf16[32,1536]{1,0:T(8,128)(2,1)S(1)} %get-tuple-element.4) | data formatting | bytes 196608
  52.6 0.6 %copy.17 = bf16[128,2,128]{2,1,0:T(2,128)(2,1)} copy(bf16[128,2,128]{2,1,0:T(2,128)(2,1)S(1)} %get-tuple-element.5) | data formatting | bytes 131072
